TPU v7x, 128 devices: a whole 4x4x4 slice. The times are simulated.
128 devices in a mesh: dp: 32 (over y, x, core), tensor: 4 (over z).
Axes of the slice: x: 4, y: 4, z: 4, core: 2. Of those that a mesh axis runs over, the one named last changes fastest.
Arguments:
- tokens: bfloat16 [20480, 1152], P(('dp', 'tensor')), may hold values from -6 to 6
- cotangent: bfloat16 [20480, 1152], P(('dp', 'tensor')), may hold values from -24 to 24
- segment_ids: int32 [32, 640], P('dp'), may hold values from 0 to 3, as said below
- positions: int32 [32, 640], P('dp'), may hold values from 0 to 1999, as said below
- w_query: bfloat16 [1152, 1024], P('dp', 'tensor')
- w_key: bfloat16 [1152, 256], P('dp')
- w_value: bfloat16 [1152, 256], P('dp'), may hold values from -0.1875 to 0.1875
- w_out: bfloat16 [1024, 1152], P('tensor', 'dp'), may hold values from -0.1875 to 0.1875
- w_gate: bfloat16 [1152, 6912], P('dp', 'tensor'), may hold values from -0.1875 to 0.1875
- w_up: bfloat16 [1152, 6912], P('dp', 'tensor'), may hold values from -0.1875 to 0.1875
- w_down: bfloat16 [6912, 1152], P('tensor', 'dp'), may hold values from -0.078125 to 0.078125
- prenorm_attn: bfloat16 [1152], P('dp'), may hold values from 0.099609375 to 1.8984375
- postnorm_attn: bfloat16 [1152], P('dp'), may hold values from 0.099609375 to 1.8984375
- prenorm_ffw: bfloat16 [1152], P('dp'), may hold values from 0.099609375 to 1.8984375
- postnorm_ffw: bfloat16 [1152], P('dp'), may hold values from 0.099609375 to 1.8984375
- query_norm: bfloat16 [256], P('dp'), may hold values from 0.6 to 5
- key_norm: bfloat16 [256], P('dp'), may hold values from 0.6 to 5
Outputs:
- layer_out: bfloat16 [20480, 1152], P(('dp', 'tensor'))
- grad_tokens: float32 [20480, 1152], P(('dp', 'tensor'))
- grad_query: float32 [1152, 1024], P('dp', 'tensor')
- grad_key: float32 [1152, 256], P('dp')
- grad_value: float32 [1152, 256], P('dp')
- grad_output: float32 [1024, 1152], P('tensor', 'dp')
- grad_gate: float32 [1152, 6912], P('dp', 'tensor')
- grad_up: float32 [1152, 6912], P('dp', 'tensor')
- grad_down: float32 [6912, 1152], P('tensor', 'dp')
- grad_prenorm_attn: float32 [1152], P('dp')
- grad_postnorm_attn: float32 [1152], P('dp')
- grad_prenorm_ffw: float32 [1152], P('dp')
- grad_postnorm_ffw: float32 [1152], P('dp')
- grad_query_norm: float32 [256], P('dp')
- grad_key_norm: float32 [256], P('dp')
Inputs may be any that keep to these rules, and one draw needn't show every extreme that they name: `segment_ids`: within each sequence the numbers never fall; a document is a run of equal numbers. Within a document positions rise by one from token to token.
All inputs are finite; a program needn't handle non-finite values.
Results may differ from a plain program's by a relative error of at most 0.033.
The roundings to bfloat16 on the way count: a program that leaves them out, or rounds other values in their place, can miss the bound.
Values may be sent and summed in bfloat16 or wider, within the bound.
A program may use at most 128 MiB of HBM per device.

v0:
```python
import math
import jax
import jax.numpy as jnp
from jax import lax
from jax.sharding import PartitionSpec as P

WINDOW = 512
EPSILON = 1e-06
ROPE_BASE = 10000.0
GELU_SCALE = math.sqrt(2.0 / math.pi)
MASKED = -1e30


def normalize(inputs):
    inverse = lax.rsqrt(jnp.mean(inputs * inputs, axis=-1, keepdims=True) + EPSILON)
    return (inputs * inverse, inverse)


def normalize_back(grad_hat, normed, inverse):
    return inverse * (grad_hat - normed * jnp.mean(grad_hat * normed, axis=-1, keepdims=True))


def rotary_tables(places, width):
    half = width // 2
    freqs = ROPE_BASE ** (-(jnp.arange(half, dtype=jnp.float32) * 2.0) / width)
    angles = places.astype(jnp.float32)[:, None] * freqs[None, :]
    return (jnp.cos(angles), jnp.sin(angles))


def rotate(inputs, cosine, sine):
    half = inputs.shape[-1] // 2
    first = inputs[:, :half]
    second = inputs[:, half:]
    return jnp.concatenate(
        [first * cosine - second * sine, second * cosine + first * sine], axis=-1
    )


def gelu_parts(inputs):
    inner = GELU_SCALE * (inputs + 0.044715 * inputs * inputs * inputs)
    tangent = jnp.tanh(inner)
    result = 0.5 * inputs * (1.0 + tangent)
    slope = 0.5 * (1.0 + tangent) + 0.5 * inputs * (1.0 - tangent * tangent) * GELU_SCALE * (
        1.0 + 3.0 * 0.044715 * inputs * inputs
    )
    return (result, slope)


def window_mask(segments):
    length = segments.shape[0]
    places = jnp.arange(length, dtype=jnp.int32)
    offset = places[:, None] - places[None, :]
    same = segments[:, None] == segments[None, :]
    return same & (offset >= 0) & (offset < WINDOW)


def contract_rows(left, right):
    return lax.dot_general(
        left, right, (((0,), (0,)), ((), ())), preferred_element_type=jnp.float32
    )


def contract_cols(left, right):
    return lax.dot_general(
        left, right, (((1,), (1,)), ((), ())), preferred_element_type=jnp.float32
    )


def attend_scores(queries, keys, allowed, scale):
    return jnp.where(allowed, contract_cols(queries, keys) * scale, MASKED)


def attend_forward(queries, keys, values, allowed, scale):
    scores = attend_scores(queries, keys, allowed, scale)
    top = jnp.max(scores, axis=-1, keepdims=True)
    totals = jnp.sum(jnp.exp(scores - top), axis=-1, keepdims=True)
    logsum = top + jnp.log(totals)
    probs = jnp.exp(scores - logsum).astype(jnp.bfloat16)
    return (jnp.dot(probs, values, preferred_element_type=jnp.float32), logsum)


def attend_backward(queries, keys, values, allowed, scale, logsum, grad_heads):
    probs = jnp.exp(attend_scores(queries, keys, allowed, scale) - logsum)
    grad_values = contract_rows(probs.astype(jnp.bfloat16), grad_heads)
    grad_probs = contract_cols(grad_heads, values)
    centre = jnp.sum(probs * grad_probs, axis=-1, keepdims=True)
    grad_scores = (probs * (grad_probs - centre) * scale).astype(jnp.bfloat16)
    grad_queries = jnp.dot(grad_scores, keys, preferred_element_type=jnp.float32)
    grad_keys = contract_rows(grad_scores, queries)
    return (grad_queries, grad_keys, grad_values)


def local(
    tokens,
    cotangent,
    segment_ids,
    positions,
    w_query,
    w_key,
    w_value,
    w_out,
    w_gate,
    w_up,
    w_down,
    prenorm_attn,
    postnorm_attn,
    prenorm_ffw,
    postnorm_ffw,
    query_norm,
    key_norm,
):
    residual = tokens.astype(jnp.float32)
    attn_mats = (
        lax.all_gather(w_query, "dp", axis=0, tiled=True),
        lax.all_gather(w_key, "dp", axis=0, tiled=True),
        lax.all_gather(w_value, "dp", axis=0, tiled=True),
        lax.all_gather(w_out, "dp", axis=1, tiled=True),
        lax.all_gather(prenorm_attn, "dp", axis=0, tiled=True),
        lax.all_gather(postnorm_attn, "dp", axis=0, tiled=True),
        lax.all_gather(query_norm, "dp", axis=0, tiled=True),
        lax.all_gather(key_norm, "dp", axis=0, tiled=True),
    )
    full_query, full_key, full_value, full_out = (
        attn_mats[0],
        attn_mats[1],
        attn_mats[2],
        attn_mats[3],
    )
    gain_in = attn_mats[4].astype(jnp.float32)
    gain_post = attn_mats[5].astype(jnp.float32)
    gain_query = attn_mats[6].astype(jnp.float32)
    gain_key = attn_mats[7].astype(jnp.float32)
    normed_in, inverse_in = normalize(residual)
    attn_rows = lax.all_gather(
        (normed_in * gain_in).astype(jnp.bfloat16), "tensor", axis=0, tiled=True
    )
    width = full_key.shape[1]
    scale = 1.0 / math.sqrt(width)
    cosine, sine = rotary_tables(positions.reshape(-1), width)
    masks = [window_mask(segment_ids[0])]
    key_hat, key_inverse = normalize(
        jnp.dot(attn_rows, full_key, preferred_element_type=jnp.float32)
    )
    keys = rotate(key_hat * gain_key, cosine, sine).astype(jnp.bfloat16)
    values = jnp.dot(attn_rows, full_value, preferred_element_type=jnp.float32).astype(jnp.bfloat16)
    query_hat, query_inverse = normalize(
        jnp.dot(attn_rows, full_query, preferred_element_type=jnp.float32)
    )
    queries = rotate(query_hat * gain_query, cosine, sine).astype(jnp.bfloat16)
    sequence = 0
    piece, logsum = attend_forward(queries, keys, values, masks[sequence], scale)
    logsums = logsum
    saved = [(query_hat, query_inverse, queries, logsums)]
    heads_out = piece.astype(jnp.bfloat16)
    attn_sum = lax.psum_scatter(
        jnp.dot(heads_out, full_out, preferred_element_type=jnp.float32),
        "tensor",
        scatter_dimension=0,
        tiled=True,
    )
    attn_hat, attn_inverse = normalize(attn_sum)
    hidden = residual + attn_hat * gain_post
    ffw_mats = (
        lax.all_gather(w_gate, "dp", axis=0, tiled=True),
        lax.all_gather(w_up, "dp", axis=0, tiled=True),
        lax.all_gather(w_down, "dp", axis=1, tiled=True),
        lax.all_gather(prenorm_ffw, "dp", axis=0, tiled=True),
        lax.all_gather(postnorm_ffw, "dp", axis=0, tiled=True),
    )
    full_gate, full_up, full_down = (ffw_mats[0], ffw_mats[1], ffw_mats[2])
    gain_ffw_in = ffw_mats[3].astype(jnp.float32)
    gain_ffw_post = ffw_mats[4].astype(jnp.float32)
    mid_hat, mid_inverse = normalize(hidden)
    ffw_rows = lax.all_gather(
        (mid_hat * gain_ffw_in).astype(jnp.bfloat16), "tensor", axis=0, tiled=True
    )
    gate = jnp.dot(ffw_rows, full_gate, preferred_element_type=jnp.float32)
    upward = jnp.dot(ffw_rows, full_up, preferred_element_type=jnp.float32)
    gelu_value, gelu_slope = gelu_parts(gate)
    act = (gelu_value * upward).astype(jnp.bfloat16)
    ffw_sum = lax.psum_scatter(
        jnp.dot(act, full_down, preferred_element_type=jnp.float32),
        "tensor",
        scatter_dimension=0,
        tiled=True,
    )
    ffw_hat, ffw_inverse = normalize(ffw_sum)
    layer_out = (hidden + ffw_hat * gain_ffw_post).astype(jnp.bfloat16)
    back_mats = (
        lax.all_gather(w_query, "dp", axis=0, tiled=True),
        lax.all_gather(w_key, "dp", axis=0, tiled=True),
        lax.all_gather(w_value, "dp", axis=0, tiled=True),
        lax.all_gather(w_out, "dp", axis=1, tiled=True),
        lax.all_gather(w_gate, "dp", axis=0, tiled=True),
        lax.all_gather(w_up, "dp", axis=0, tiled=True),
        lax.all_gather(w_down, "dp", axis=1, tiled=True),
    )
    back_query, back_key, back_value, back_out = (
        back_mats[0],
        back_mats[1],
        back_mats[2],
        back_mats[3],
    )
    back_gate, back_up, back_down = (back_mats[4], back_mats[5], back_mats[6])
    grad_out = cotangent.astype(jnp.float32)
    grad_post_ffw = jnp.sum(grad_out * ffw_hat, axis=0)
    grad_ffw_local = normalize_back(grad_out * gain_ffw_post, ffw_hat, ffw_inverse).astype(
        jnp.bfloat16
    )
    grad_ffw = lax.all_gather(grad_ffw_local, "tensor", axis=0, tiled=True)
    grad_down_turned = contract_rows(grad_ffw, act)
    grad_act = contract_cols(grad_ffw, back_down)
    grad_gate_in = (grad_act * upward * gelu_slope).astype(jnp.bfloat16)
    grad_up_in = (grad_act * gelu_value).astype(jnp.bfloat16)
    grad_gate = contract_rows(ffw_rows, grad_gate_in)
    grad_up = contract_rows(ffw_rows, grad_up_in)
    ffw_in_shards = (
        lax.psum_scatter(
            grad_gate.astype(jnp.bfloat16), "dp", scatter_dimension=0, tiled=True
        ).astype(jnp.float32),
        lax.psum_scatter(
            grad_up.astype(jnp.bfloat16), "dp", scatter_dimension=0, tiled=True
        ).astype(jnp.float32),
    )
    grad_mid = lax.psum_scatter(
        contract_cols(grad_gate_in, back_gate) + contract_cols(grad_up_in, back_up),
        "tensor",
        scatter_dimension=0,
        tiled=True,
    )
    grad_pre_ffw = jnp.sum(grad_mid * mid_hat, axis=0)
    grad_hidden = grad_out + normalize_back(grad_mid * gain_ffw_in, mid_hat, mid_inverse)
    grad_post_attn = jnp.sum(grad_hidden * attn_hat, axis=0)
    grad_attn_local = normalize_back(grad_hidden * gain_post, attn_hat, attn_inverse).astype(
        jnp.bfloat16
    )
    grad_attn = lax.all_gather(grad_attn_local, "tensor", axis=0, tiled=True)
    grad_out_turned = contract_rows(grad_attn, heads_out)
    grad_heads = contract_cols(grad_attn, back_out).astype(jnp.bfloat16)
    which = 0
    query_hat, query_inverse, queries, logsum = saved[which]
    sequence = 0
    grad_queries, grad_keys, grad_values = attend_backward(
        queries, keys, values, masks[sequence], scale, logsum, grad_heads
    )
    grad_query_turned = rotate(grad_queries, cosine, -sine)
    grad_query_norm = jnp.sum(grad_query_turned * query_hat, axis=0)
    query_in = normalize_back(grad_query_turned * gain_query, query_hat, query_inverse).astype(
        jnp.bfloat16
    )
    grad_key_turned = rotate(grad_keys, cosine, -sine)
    grad_key_norm = jnp.sum(grad_key_turned * key_hat, axis=0)
    key_in = normalize_back(grad_key_turned * gain_key, key_hat, key_inverse).astype(jnp.bfloat16)
    value_in = grad_values.astype(jnp.bfloat16)
    query_blocks = contract_rows(attn_rows, query_in)
    grad_key = contract_rows(attn_rows, key_in)
    grad_value = contract_rows(attn_rows, value_in)
    query_ins = [query_in]
    key_ins = [key_in]
    value_ins = [value_in]
    which = 0
    total = contract_cols(query_ins[which], back_query)
    total = total + contract_cols(key_ins[which], back_key)
    total = total + contract_cols(value_ins[which], back_value)
    grad_in_rows = lax.psum_scatter(
        total.astype(jnp.bfloat16), "tensor", scatter_dimension=0, tiled=True
    ).astype(jnp.float32)
    grad_pre_attn = jnp.sum(grad_in_rows * normed_in, axis=0)
    grad_tokens = grad_hidden + normalize_back(grad_in_rows * gain_in, normed_in, inverse_in)
    rest = (
        lax.psum_scatter(
            query_blocks.astype(jnp.bfloat16), "dp", scatter_dimension=0, tiled=True
        ).astype(jnp.float32),
        lax.psum_scatter(
            grad_key.astype(jnp.bfloat16), "dp", scatter_dimension=0, tiled=True
        ).astype(jnp.float32),
        lax.psum_scatter(
            grad_value.astype(jnp.bfloat16), "dp", scatter_dimension=0, tiled=True
        ).astype(jnp.float32),
        lax.psum_scatter(
            grad_out_turned.astype(jnp.bfloat16), "dp", scatter_dimension=0, tiled=True
        ).astype(jnp.float32),
        lax.psum_scatter(
            grad_down_turned.astype(jnp.bfloat16), "dp", scatter_dimension=0, tiled=True
        ).astype(jnp.float32),
        lax.psum_scatter(
            grad_pre_attn.astype(jnp.bfloat16), "dp", scatter_dimension=0, tiled=True
        ).astype(jnp.float32),
        lax.psum_scatter(
            grad_post_attn.astype(jnp.bfloat16), "dp", scatter_dimension=0, tiled=True
        ).astype(jnp.float32),
        lax.psum_scatter(
            grad_pre_ffw.astype(jnp.bfloat16), "dp", scatter_dimension=0, tiled=True
        ).astype(jnp.float32),
        lax.psum_scatter(
            grad_post_ffw.astype(jnp.bfloat16), "dp", scatter_dimension=0, tiled=True
        ).astype(jnp.float32),
        lax.psum_scatter(
            grad_query_norm.astype(jnp.bfloat16), "dp", scatter_dimension=0, tiled=True
        ).astype(jnp.float32),
        lax.psum_scatter(
            grad_key_norm.astype(jnp.bfloat16), "dp", scatter_dimension=0, tiled=True
        ).astype(jnp.float32),
    )
    shared = (
        lax.psum(rest[1].astype(jnp.bfloat16), "tensor").astype(jnp.float32),
        lax.psum(rest[2].astype(jnp.bfloat16), "tensor").astype(jnp.float32),
        lax.psum(rest[5].astype(jnp.bfloat16), "tensor").astype(jnp.float32),
        lax.psum(rest[6].astype(jnp.bfloat16), "tensor").astype(jnp.float32),
        lax.psum(rest[7].astype(jnp.bfloat16), "tensor").astype(jnp.float32),
        lax.psum(rest[8].astype(jnp.bfloat16), "tensor").astype(jnp.float32),
        lax.psum(rest[9].astype(jnp.bfloat16), "tensor").astype(jnp.float32),
        lax.psum(rest[10].astype(jnp.bfloat16), "tensor").astype(jnp.float32),
    )
    return (
        layer_out,
        grad_tokens,
        rest[0],
        shared[0],
        shared[1],
        rest[3].T,
        ffw_in_shards[0],
        ffw_in_shards[1],
        rest[4].T,
        shared[2],
        shared[3],
        shared[4],
        shared[5],
        shared[6],
        shared[7],
    )


def solution(mesh):
    placed = (
        P(("dp", "tensor"), None),
        P(("dp", "tensor"), None),
        P("dp", None),
        P("dp", None),
        P("dp", "tensor"),
        P("dp", None),
        P("dp", None),
        P("tensor", "dp"),
        P("dp", "tensor"),
        P("dp", "tensor"),
        P("tensor", "dp"),
        P("dp"),
        P("dp"),
        P("dp"),
        P("dp"),
        P("dp"),
        P("dp"),
    )
    return jax.shard_map(
        local,
        mesh=mesh,
        in_specs=placed,
        out_specs=(
            P(("dp", "tensor"), None),
            P(("dp", "tensor"), None),
            P("dp", "tensor"),
            P("dp", None),
            P("dp", None),
            P("tensor", "dp"),
            P("dp", "tensor"),
            P("dp", "tensor"),
            P("tensor", "dp"),
            P("dp"),
            P("dp"),
            P("dp"),
            P("dp"),
            P("dp"),
            P("dp"),
        ),
        check_vma=False,
    )
```

profile of v0, /device:TPU:0, one launch (start us, length us, event | category | flops | bytes accessed | tf_op | source)
XLA Modules:
  0.0 971.6 jit_solution(9938166193788936195)
XLA Ops:
  15.8 128.5 %all-reduce.27 = (bf16[1152]{0:T(1024)(128)(2,1)S(1)}, bf16[256]{0:T(256)(128)(2,1)S(1)}, bf16[256]{0:T(256)(128)(2,1)S(1)}, bf16[1152]{0:T(1024)(128)(2,1)S(1)}...) all-reduce(bf16[1152]{0:T(1024)(128)(2,1)S(1)} %dynamic-update-slic, ...), channel_id=1, replica_groups=mesh['dp'=32,'tensor'=4] {'dp'}, use_global_device_ids=true, to_apply=%add | all-reduce | flops 5120 | bytes 20480
  147.5 22.5 %all-gather.2 = bf16[32,36,256]{2,1,0:T(8,128)(2,1)S(1)} all-gather(bf16[1,36,256]{2,1,0:T(8,128)(2,1)} %bitcast.84), channel_id=1, replica_groups=mesh['dp'=32,'tensor'=4] {'dp'}, dimensions={0}, use_global_device_ids=true | all-gather | bytes 608256 | tf_op jit(solution)/shard_map/all_gather | solution.py:116
  170.2 24.3 %all-gather.1 = bf16[32,36,256]{2,1,0:T(8,128)(2,1)S(1)} all-gather(bf16[1,36,256]{2,1,0:T(8,128)(2,1)S(1)} %bitcast.85), channel_id=1, replica_groups=mesh['dp'=32,'tensor'=4] {'dp'}, dimensions={0}, use_global_device_ids=true | all-gather | bytes 608256 | tf_op jit(solution)/shard_map/all_gather | solution.py:115
  194.7 22.6 %all-gather = bf16[32,36,256]{2,1,0:T(8,128)(2,1)S(1)} all-gather(bf16[1,36,256]{2,1,0:T(8,128)(2,1)S(1)} %bitcast.86), channel_id=1, replica_groups=mesh['dp'=32,'tensor'=4] {'dp'}, dimensions={0}, use_global_device_ids=true | all-gather | bytes 608256 | tf_op jit(solution)/shard_map/all_gather | solution.py:114
  217.5 24.6 %all-gather.3 = bf16[32,36,256]{2,1,0:T(8,128)(2,1)S(1)} all-gather(bf16[1,36,256]{2,1,0:T(8,128)(2,1)S(1)} %bitcast.87), channel_id=1, replica_groups=mesh['dp'=32,'tensor'=4] {'dp'}, dimensions={0}, use_global_device_ids=true | all-gather | bytes 608256 | tf_op jit(solution)/shard_map/all_gather | solution.py:117
  254.9 34.6 %reduce-scatter.19.cloned.1.call-done = f32[160,1152]{1,0:T(8,128)} async-done(((f32[640,1152]{1,0:T(8,128)}), f32[160,1152]{1,0:T(8,128)}) %reduce-scatter.19.cloned.1.call-update) | async-done | bytes 737296 | tf_op jit(solution)/shard_map/reduce_scatter | solution.py:155
  293.6 8.0 all-gather.23.cloned.1.call-done
  301.6 7.3 reshape.160
  308.9 40.7 %all-gather.25.cloned.1.call-done = bf16[32,36,1728]{2,1,0:T(8,128)(2,1)} async-done(((bf16[1,36,1728]{2,1,0:T(8,128)(2,1)}), bf16[32,36,1728]{2,1,0:T(8,128)(2,1)}) %all-gather.25.cloned.1.call-update) | async-done | bytes 3981328 | tf_op jit(solution)/shard_map/all_gather | solution.py:165
  349.5 7.3 reshape.162
  356.8 40.7 %all-gather.27.cloned.1.call-done = bf16[32,36,1728]{2,1,0:T(8,128)(2,1)} async-done(((bf16[1,36,1728]{2,1,0:T(8,128)(2,1)}), bf16[32,36,1728]{2,1,0:T(8,128)(2,1)}) %all-gather.27.cloned.1.call-update) | async-done | bytes 3981328 | tf_op jit(solution)/shard_map/all_gather | solution.py:166
  397.5 7.3 reshape.164
  404.8 20.2 %all-gather.17.cloned.1.call-done = bf16[640,1152]{1,0:T(8,128)(2,1)} async-done(((bf16[160,1152]{1,0:T(8,128)(2,1)}), bf16[640,1152]{1,0:T(8,128)(2,1)}) %all-gather.17.cloned.1.call-update) | async-done | bytes 1474576 | tf_op jit(solution)/shard_map/all_gather | solution.py:174
  425.0 6.5 fusion.77
  431.5 6.7 multiply_convert_fusion.1
  439.7 4.8 fusion.78
  444.7 36.9 %reduce-scatter.21.cloned.1.call-done = f32[160,1152]{1,0:T(8,128)} async-done(((f32[640,1152]{1,0:T(8,128)}), f32[160,1152]{1,0:T(8,128)}) %reduce-scatter.21.cloned.1.call-update) | async-done | bytes 737296 | tf_op jit(solution)/shard_map/reduce_scatter | solution.py:181
  485.6 25.6 %all-gather.19.cloned.1.call-done = bf16[640,1152]{1,0:T(8,128)(2,1)} async-done(((bf16[160,1152]{1,0:T(8,128)(2,1)}), bf16[640,1152]{1,0:T(8,128)(2,1)}) %all-gather.19.cloned.1.call-update) | async-done | bytes 1474576 | tf_op jit(solution)/shard_map/all_gather | solution.py:210
  511.2 10.2 %multiply_convert_fusion = (bf16[640,1728]{0,1:T(8,128)(2,1)S(1)}, bf16[640,1728]{0,1:T(8,128)(2,1)S(1)}) fusion(f32[640,1728]{0,1:T(8,128)} %copy-done.52, f32[640,1728]{0,1:T(8,128)} %get-tuple-element.90, bf16[640,1152]{1,0:T(8,128)(2,1)} %all-gather.19.cloned.1.call-done, bf16[1152,1728]{1,0:T(8,128)(2,1)} %reshape.164), kind=kOutput, calls=%fused_computation.12 | convolution fusion | flops 2573475840 | bytes 18726912 | tf_op jit(solution)/shard_map/dot_general | solution.py:64
  521.5 3.2 fusion.79
  525.2 4.9 convolution_add_fusion.2
  530.2 37.1 %reduce-scatter.23.cloned.1.call-done = f32[160,1152]{1,0:T(8,128)} async-done(((f32[640,1152]{1,0:T(8,128)}), f32[160,1152]{1,0:T(8,128)}) %reduce-scatter.23.cloned.1.call-update) | async-done | bytes 737296 | tf_op jit(solution)/shard_map/reduce_scatter | solution.py:225
  572.7 7.7 convolution_convert_fusion.2
  580.4 5.4 convolution_convert_fusion.1
  585.8 12.3 %all-gather.21.cloned.1.call-done = bf16[640,1152]{1,0:T(8,128)(2,1)} async-done(((bf16[160,1152]{1,0:T(8,128)(2,1)}), bf16[640,1152]{1,0:T(8,128)(2,1)}) %all-gather.21.cloned.1.call-update) | async-done | bytes 1474576 | tf_op jit(solution)/shard_map/all_gather | solution.py:237
  610.4 7.6 convolution_convert_fusion
  623.2 98.4 %fusion.73 = (bf16[40,256]{1,0:T(8,128)(2,1)S(1)}, bf16[40,256]{1,0:T(8,128)(2,1)S(1)}, bf16[40,256]{1,0:T(8,128)(2,1)S(1)}, bf16[40,256]{1,0:T(8,128)(2,1)S(1)}...) fusion(bf16[1152,256]{1,0:T(8,128)(2,1)S(1)} %convolution_convert_fusion.6, ...), kind=kCustom, calls=%all-reduce-scatter.7 | all-reduce-scatter fusion | flops 7946241 | bytes 14800384
  724.3 5.6 collective-permute-start.23
  732.1 5.3 collective-permute-start.7
  737.5 3.0 collective-permute-start.11
  740.5 5.2 collective-permute-start.15
  749.1 5.1 collective-permute-start.6
  754.3 4.0 collective-permute-start.5
  759.8 3.3 collective-permute-start.10
  763.1 3.7 collective-permute-start.9
  766.8 2.5 collective-permute-start.14
  769.4 3.6 collective-permute-start.13
  773.1 2.3 collective-permute-start.12
  778.4 2.5 collective-permute-start.8
  782.9 2.5 collective-permute-start.17
  787.1 2.4 collective-permute-start.22
  794.0 2.5 collective-permute-start.20
  798.0 2.9 collective-permute-start.25
  800.9 2.4 collective-permute-start.24
  806.4 2.5 concatenate.23
  809.4 3.2 concatenate.24
  816.3 123.9 %all-reduce.26 = (bf16[1152]{0:T(1024)(128)(2,1)S(1)}, bf16[1152]{0:T(1024)(128)(2,1)S(1)}, bf16[1152]{0:T(1024)(128)(2,1)S(1)}, bf16[1152]{0:T(1024)(128)(2,1)S...) all-reduce(bf16[1152]{0:T(1024)(128)(2,1)S(1)} %get-tuple-element.2, ...), channel_id=13, replica_groups=mesh['dp'=32,'tensor'=4] {'dp'}, use_global_device_ids=true, to_apply=%region_29.30.clone | all-reduce | flops 5120 | bytes 20480
  940.7 16.3 %all-reduce.28 = (bf16[36,256]{1,0:T(8,128)(2,1)S(1)}, bf16[36,256]{1,0:T(8,128)(2,1)S(1)}, bf16[36]{0:T(256)(128)(2,1)S(1)}, bf16[36]{0:T(256)(128)(2,1)S(1)}, ...) all-reduce(bf16[36,256]{1,0:T(8,128)(2,1)S(1)} %constant_dynamic-sl, ...), channel_id=1, replica_groups=mesh['dp'=32,'tensor'=4] {'tensor'}, use_global_device_ids=true, to_apply=%region_21.22 | all-reduce | flops 18592 | bytes 74368 | tf_op jit(solution)/shard_map/psum | solution.py:306
  (289 shorter events, 90.0 us)
Async XLA Ops:
  8.0 162.2 %copy-start.38 = (bf16[36,256]{1,0:T(8,128)(2,1)S(1)}, bf16[36,256]{1,0:T(8,128)(2,1)}, u32[]{:S(2)}) copy-start(bf16[36,256]{1,0:T(8,128)(2,1)} %param.22) | copy-start | bytes 55300
  8.0 234.3 %all-gather.15.cloned.1.call-start = ((), (), s32[]{:S(2)}) async-start(), calls=%async_computation.4 | async-start | bytes 1843200 | tf_op jit(solution)/shard_map/all_gather | solution.py:134
  147.4 47.3 %copy-start.39 = (bf16[36,256]{1,0:T(8,128)(2,1)S(1)}, bf16[36,256]{1,0:T(8,128)(2,1)}, u32[]{:S(2)}) copy-start(bf16[36,256]{1,0:T(8,128)(2,1)} %param.21) | copy-start | bytes 55300
  147.5 142.0 %reduce-scatter.19.cloned.1.call-start = ((), (), s32[]{:S(2)}) async-start(), calls=%async_computation.5 | async-start | bytes 3686400 | tf_op jit(solution)/shard_map/reduce_scatter | solution.py:155
  170.2 78.1 %copy-start.20 = (bf16[1152,256]{1,0:T(8,128)(2,1)}, bf16[1152,256]{1,0:T(8,128)(2,1)S(1)}, u32[]{:S(2)}) copy-start(bf16[1152,256]{1,0:T(8,128)(2,1)S(1)} %reshape.156) | copy-start | bytes 1769476
  170.2 47.3 %copy-start.40 = (bf16[256,36]{0,1:T(8,128)(2,1)S(1)}, bf16[256,36]{0,1:T(8,128)(2,1)}, u32[]{:S(2)}) copy-start(bf16[256,36]{0,1:T(8,128)(2,1)} %param.24) | copy-start | bytes 55300
  194.6 49.9 %copy-start.11 = (bf16[1152,256]{1,0:T(8,128)(2,1)}, bf16[1152,256]{1,0:T(8,128)(2,1)S(1)}, u32[]{:S(2)}) copy-start(bf16[1152,256]{1,0:T(8,128)(2,1)S(1)} %reshape.154) | copy-start | bytes 1769476
  194.7 47.5 %copy-start.44 = (s32[1,640]{1,0:T(1,128)S(1)}, s32[1,640]{1,0:T(1,128)}, u32[]{:S(2)}) copy-start(s32[1,640]{1,0:T(1,128)} %param.19) | copy-start | bytes 7684
  194.7 47.6 %copy-start.45 = (s32[1,640]{1,0:T(1,128)S(1)}, s32[1,640]{1,0:T(1,128)}, u32[]{:S(2)}) copy-start(s32[1,640]{1,0:T(1,128)} %param.20) | copy-start | bytes 7684
  194.7 50.7 %copy-start.42 = (f32[256]{0:T(256)}, f32[256]{0:T(256)S(1)}, u32[]{:S(2)}) copy-start(f32[256]{0:T(256)S(1)} %convert_element_type.184) | copy-start | bytes 3076
  253.1 48.5 %all-gather.23.cloned.1.call-start = ((), (), s32[]{:S(2)}) async-start(), calls=%async_computation.12 | async-start | bytes 4730880 | tf_op jit(solution)/shard_map/all_gather | solution.py:164
  253.6 95.9 %all-gather.25.cloned.1.call-start = ((), (), s32[]{:S(2)}) async-start(), calls=%async_computation.13 | async-start | bytes 4730880 | tf_op jit(solution)/shard_map/all_gather | solution.py:165
  254.2 143.3 %all-gather.27.cloned.1.call-start = ((), (), s32[]{:S(2)}) async-start(), calls=%async_computation.14 | async-start | bytes 4730880 | tf_op jit(solution)/shard_map/all_gather | solution.py:166
  254.8 170.2 %all-gather.17.cloned.1.call-start = ((), (), s32[]{:S(2)}) async-start(), calls=%async_computation.6 | async-start | bytes 1843200 | tf_op jit(solution)/shard_map/all_gather | solution.py:174
  293.1 188.5 %reduce-scatter.21.cloned.1.call-start = ((), (), s32[]{:S(2)}) async-start(), calls=%async_computation.7 | async-start | bytes 3686400 | tf_op jit(solution)/shard_map/reduce_scatter | solution.py:181
  444.5 66.7 %all-gather.19.cloned.1.call-start = ((), (), s32[]{:S(2)}) async-start(), calls=%async_computation.8 | async-start | bytes 1843200 | tf_op jit(solution)/shard_map/all_gather | solution.py:210
  485.6 81.7 %reduce-scatter.23.cloned.1.call-start = ((), (), s32[]{:S(2)}) async-start(), calls=%async_computation.9 | async-start | bytes 3686400 | tf_op jit(solution)/shard_map/reduce_scatter | solution.py:225
  530.2 67.8 %all-gather.21.cloned.1.call-start = ((), (), s32[]{:S(2)}) async-start(), calls=%async_computation.10 | async-start | bytes 1843200 | tf_op jit(solution)/shard_map/all_gather | solution.py:237
  572.4 242.5 %reduce-scatter.25.cloned.1.call-start = ((), (), s32[]{:S(2)}) async-start(), calls=%async_computation.11 | async-start | bytes 1843200 | tf_op jit(solution)/shard_map/reduce_scatter | solution.py:265
  721.7 36.6 %collective-permute-start.2 = (bf16[40,256]{1,0:T(8,128)(2,1)S(1)}, bf16[40,256]{1,0:T(8,128)(2,1)S(1)}, u32[]{:S(2)}, u32[]{:S(2)}) collective-permute-start(bf16[40,256]{1,0:T(8,128)(2,1)S(1)} %get-tuple-element.54), channel_id=1, source_target_pairs={{0,12},{4,16},{8,20},{12,24},{16,28},{20,32},{24,36},{28,40},{32,4... | collective-permute-start | bytes 61448
  723.0 26.1 %collective-permute-start.19 = (bf16[4,1728]{1,0:T(4,128)(2,1)S(1)}, bf16[4,1728]{1,0:T(4,128)(2,1)S(1)}, u32[]{:S(2)}, u32[]{:S(2)}) collective-permute-start(bf16[4,1728]{1,0:T(4,128)(2,1)S(1)} %slice.44), channel_id=1, source_target_pairs={{0,16},{4,20},{8,24},{12,28},{16,32},{20,36},{24,40},{28,44},{32,4... | collective-permute-start | bytes 41480
  724.3 30.0 %collective-permute-start.23 = (bf16[4,1728]{1,0:T(4,128)(2,1)S(1)}, bf16[4,1728]{1,0:T(4,128)(2,1)}, u32[]{:S(2)}, u32[]{:S(2)}) collective-permute-start(bf16[4,1728]{1,0:T(4,128)(2,1)S(1)} %slice.45), channel_id=1, source_target_pairs={{0,16},{4,20},{8,24},{12,28},{16,32},{20,36},{24,40},{28,44},{32,4... | collective-permute-start | bytes 41480
  730.0 7.5 collective-permute-start.3
  732.1 8.3 collective-permute-start.7
  737.5 8.3 collective-permute-start.11
  740.5 6.5 collective-permute-start.15
  745.7 14.1 %collective-permute-start.1 = (bf16[40,256]{1,0:T(8,128)(2,1)S(1)}, bf16[40,256]{1,0:T(8,128)(2,1)S(1)}, u32[]{:S(2)}, u32[]{:S(2)}) collective-permute-start(bf16[40,256]{1,0:T(8,128)(2,1)S(1)} %get-tuple-element.54), channel_id=1, source_target_pairs={{0,8},{4,12},{8,16},{12,20},{16,24},{20,28},{24,32},{28,36},{32,40... | collective-permute-start | bytes 61448
  747.0 16.1 %collective-permute-start = (bf16[40,256]{1,0:T(8,128)(2,1)S(1)}, bf16[40,256]{1,0:T(8,128)(2,1)S(1)}, u32[]{:S(2)}, u32[]{:S(2)}) collective-permute-start(bf16[40,256]{1,0:T(8,128)(2,1)S(1)} %get-tuple-element.54), channel_id=1, source_target_pairs={{0,4},{4,8},{8,12},{12,16},{16,20},{20,24},{24,28},{28,32},{32,36}... | collective-permute-start | bytes 61448
  749.1 17.7 %collective-permute-start.6 = (bf16[40,256]{1,0:T(8,128)(2,1)S(1)}, bf16[40,256]{1,0:T(8,128)(2,1)S(1)}, u32[]{:S(2)}, u32[]{:S(2)}) collective-permute-start(bf16[40,256]{1,0:T(8,128)(2,1)S(1)} %get-tuple-element.55), channel_id=1, source_target_pairs={{0,12},{4,16},{8,20},{12,24},{16,28},{20,32},{24,36},{28,40},{32,4... | collective-permute-start | bytes 61448
  754.3 15.1 %collective-permute-start.5 = (bf16[40,256]{1,0:T(8,128)(2,1)S(1)}, bf16[40,256]{1,0:T(8,128)(2,1)S(1)}, u32[]{:S(2)}, u32[]{:S(2)}) collective-permute-start(bf16[40,256]{1,0:T(8,128)(2,1)S(1)} %get-tuple-element.55), channel_id=1, source_target_pairs={{0,8},{4,12},{8,16},{12,20},{16,24},{20,28},{24,32},{28,36},{32,40... | collective-permute-start | bytes 61448
  758.3 14.8 %collective-permute-start.4 = (bf16[40,256]{1,0:T(8,128)(2,1)S(1)}, bf16[40,256]{1,0:T(8,128)(2,1)S(1)}, u32[]{:S(2)}, u32[]{:S(2)}) collective-permute-start(bf16[40,256]{1,0:T(8,128)(2,1)S(1)} %get-tuple-element.55), channel_id=1, source_target_pairs={{0,4},{4,8},{8,12},{12,16},{16,20},{20,24},{24,28},{28,32},{32,36}... | collective-permute-start | bytes 61448
  759.8 18.7 %collective-permute-start.10 = (bf16[40,256]{1,0:T(8,128)(2,1)S(1)}, bf16[40,256]{1,0:T(8,128)(2,1)S(1)}, u32[]{:S(2)}, u32[]{:S(2)}) collective-permute-start(bf16[40,256]{1,0:T(8,128)(2,1)S(1)} %get-tuple-element.56), channel_id=1, source_target_pairs={{0,12},{4,16},{8,20},{12,24},{16,28},{20,32},{24,36},{28,40},{32,4... | collective-permute-start | bytes 61448
  763.1 17.8 %collective-permute-start.9 = (bf16[40,256]{1,0:T(8,128)(2,1)S(1)}, bf16[40,256]{1,0:T(8,128)(2,1)S(1)}, u32[]{:S(2)}, u32[]{:S(2)}) collective-permute-start(bf16[40,256]{1,0:T(8,128)(2,1)S(1)} %get-tuple-element.56), channel_id=1, source_target_pairs={{0,8},{4,12},{8,16},{12,20},{16,24},{20,28},{24,32},{28,36},{32,40... | collective-permute-start | bytes 61448
  766.8 16.0 %collective-permute-start.14 = (bf16[40,256]{1,0:T(8,128)(2,1)S(1)}, bf16[40,256]{1,0:T(8,128)(2,1)S(1)}, u32[]{:S(2)}, u32[]{:S(2)}) collective-permute-start(bf16[40,256]{1,0:T(8,128)(2,1)S(1)} %get-tuple-element.57), channel_id=1, source_target_pairs={{0,12},{4,16},{8,20},{12,24},{16,28},{20,32},{24,36},{28,40},{32,4... | collective-permute-start | bytes 61448
  769.4 16.0 %collective-permute-start.13 = (bf16[40,256]{1,0:T(8,128)(2,1)S(1)}, bf16[40,256]{1,0:T(8,128)(2,1)S(1)}, u32[]{:S(2)}, u32[]{:S(2)}) collective-permute-start(bf16[40,256]{1,0:T(8,128)(2,1)S(1)} %get-tuple-element.57), channel_id=1, source_target_pairs={{0,8},{4,12},{8,16},{12,20},{16,24},{20,28},{24,32},{28,36},{32,40... | collective-permute-start | bytes 61448
  773.1 14.1 %collective-permute-start.12 = (bf16[40,256]{1,0:T(8,128)(2,1)S(1)}, bf16[40,256]{1,0:T(8,128)(2,1)S(1)}, u32[]{:S(2)}, u32[]{:S(2)}) collective-permute-start(bf16[40,256]{1,0:T(8,128)(2,1)S(1)} %get-tuple-element.57), channel_id=1, source_target_pairs={{0,4},{4,8},{8,12},{12,16},{16,20},{20,24},{24,28},{28,32},{32,36}... | collective-permute-start | bytes 61448
  778.4 12.2 %collective-permute-start.8 = (bf16[40,256]{1,0:T(8,128)(2,1)S(1)}, bf16[40,256]{1,0:T(8,128)(2,1)S(1)}, u32[]{:S(2)}, u32[]{:S(2)}) collective-permute-start(bf16[40,256]{1,0:T(8,128)(2,1)S(1)} %get-tuple-element.56), channel_id=1, source_target_pairs={{0,4},{4,8},{8,12},{12,16},{16,20},{20,24},{24,28},{28,32},{32,36}... | collective-permute-start | bytes 61448
  781.0 13.0 %collective-permute-start.18 = (bf16[40,1728]{1,0:T(8,128)(2,1)S(1)}, bf16[40,1728]{1,0:T(8,128)(2,1)S(1)}, u32[]{:S(2)}, u32[]{:S(2)}) collective-permute-start(bf16[40,1728]{1,0:T(8,128)(2,1)S(1)} %get-tuple-element.58), channel_id=1, source_target_pairs={{0,12},{4,16},{8,20},{12,24},{16,28},{20,32},{24,36},{28,40},{32,4... | collective-permute-start | bytes 414728
  782.9 13.6 %collective-permute-start.17 = (bf16[40,1728]{1,0:T(8,128)(2,1)S(1)}, bf16[40,1728]{1,0:T(8,128)(2,1)S(1)}, u32[]{:S(2)}, u32[]{:S(2)}) collective-permute-start(bf16[40,1728]{1,0:T(8,128)(2,1)S(1)} %get-tuple-element.58), channel_id=1, source_target_pairs={{0,8},{4,12},{8,16},{12,20},{16,24},{20,28},{24,32},{28,36},{32,40... | collective-permute-start | bytes 414728
  785.4 12.6 %collective-permute-start.16 = (bf16[40,1728]{1,0:T(8,128)(2,1)S(1)}, bf16[40,1728]{1,0:T(8,128)(2,1)S(1)}, u32[]{:S(2)}, u32[]{:S(2)}) collective-permute-start(bf16[40,1728]{1,0:T(8,128)(2,1)S(1)} %get-tuple-element.58), channel_id=1, source_target_pairs={{0,4},{4,8},{8,12},{12,16},{16,20},{20,24},{24,28},{28,32},{32,36}... | collective-permute-start | bytes 414728
  787.1 13.7 %collective-permute-start.22 = (bf16[40,1728]{1,0:T(8,128)(2,1)S(1)}, bf16[40,1728]{1,0:T(8,128)(2,1)S(1)}, u32[]{:S(2)}, u32[]{:S(2)}) collective-permute-start(bf16[40,1728]{1,0:T(8,128)(2,1)S(1)} %get-tuple-element.59), channel_id=1, source_target_pairs={{0,12},{4,16},{8,20},{12,24},{16,28},{20,32},{24,36},{28,40},{32,4... | collective-permute-start | bytes 414728
  790.7 13.4 %collective-permute-start.21 = (bf16[40,1728]{1,0:T(8,128)(2,1)S(1)}, bf16[40,1728]{1,0:T(8,128)(2,1)S(1)}, u32[]{:S(2)}, u32[]{:S(2)}) collective-permute-start(bf16[40,1728]{1,0:T(8,128)(2,1)S(1)} %get-tuple-element.59), channel_id=1, source_target_pairs={{0,8},{4,12},{8,16},{12,20},{16,24},{20,28},{24,32},{28,36},{32,40... | collective-permute-start | bytes 414728
  794.0 12.4 %collective-permute-start.20 = (bf16[40,1728]{1,0:T(8,128)(2,1)S(1)}, bf16[40,1728]{1,0:T(8,128)(2,1)}, u32[]{:S(2)}, u32[]{:S(2)}) collective-permute-start(bf16[40,1728]{1,0:T(8,128)(2,1)S(1)} %get-tuple-element.59), channel_id=1, source_target_pairs={{0,4},{4,8},{8,12},{12,16},{16,20},{20,24},{24,28},{28,32},{32,36}... | collective-permute-start | bytes 414728
  796.5 12.3 %collective-permute-start.26 = (bf16[40,1728]{1,0:T(8,128)(2,1)S(1)}, bf16[40,1728]{1,0:T(8,128)(2,1)S(1)}, u32[]{:S(2)}, u32[]{:S(2)}) collective-permute-start(bf16[40,1728]{1,0:T(8,128)(2,1)S(1)} %get-tuple-element.60), channel_id=1, source_target_pairs={{0,12},{4,16},{8,20},{12,24},{16,28},{20,32},{24,36},{28,40},{32,4... | collective-permute-start | bytes 414728
  798.0 10.9 %collective-permute-start.25 = (bf16[40,1728]{1,0:T(8,128)(2,1)S(1)}, bf16[40,1728]{1,0:T(8,128)(2,1)}, u32[]{:S(2)}, u32[]{:S(2)}) collective-permute-start(bf16[40,1728]{1,0:T(8,128)(2,1)S(1)} %get-tuple-element.60), channel_id=1, source_target_pairs={{0,8},{4,12},{8,16},{12,20},{16,24},{20,28},{24,32},{28,36},{32,40... | collective-permute-start | bytes 414728
  800.9 8.6 collective-permute-start.24
  804.1 4.7 collective-permute-start.27
  806.3 155.0 %copy-start.7 = (f32[160,1152]{1,0:T(8,128)S(1)}, f32[160,1152]{1,0:T(8,128)}, u32[]{:S(2)}) copy-start(f32[160,1152]{1,0:T(8,128)} %copy-done.6) | copy-start | bytes 2211844
  (48 other events, 307.0 us)
Sparse Core Ops, SparseCore 0:
  147.6 23.1 all-gather.14
  253.2 36.2 reduce-scatter.18
  444.6 36.9 reduce-scatter.20
  485.7 25.4 all-gather.18
  530.3 36.9 reduce-scatter.22
  572.5 25.4 all-gather.20
  610.5 25.3 reduce-scatter.24
Sparse Core Ops, SparseCore 1:
  255.9 45.7 all-gather.22
  303.8 45.7 all-gather.24
  351.7 45.7 all-gather.26
  399.8 25.1 all-gather.16
where the time goes:
time: 980 us; the launch traced here: 972 us
  blocking collectives  461 us (47%)
  waiting for transfers between devices  258 us (26%)
  starting transfers between devices  78.2 us (8%)
  matrix products  76 us (8%)
  local copies, waits for them, and re-layouts  45.5 us (5%)
  other arithmetic  32 us (3%)
  between operations  21 us (2%)
    unnamed x3, blocking collectives  351 us
    unnamed x28, starting transfers between devices  76.9 us
    unnamed x156, local copies, waits for them, and re-layouts  45.5 us
    all_gather x1, waiting for transfers between devices, local(): lax.all_gather(w_down, 'dp', axis=1, tiled=True)  40.7 us
    all_gather x1, waiting for transfers between devices, local(): lax.all_gather(w_up, 'dp', axis=0, tiled=True)  40.7 us
    reduce_scatter x1, waiting for transfers between devices, local(): lax.psum_scatter(contract_cols(grad_gate_in, back_gate) + contract_cols(g...  37.1 us
    reduce_scatter x1, waiting for transfers between devices, local(): lax.psum_scatter(jnp.dot(act, full_down, preferred_element_type=jnp.float...  36.9 us
    reduce_scatter x1, waiting for transfers between devices, local(): lax.psum_scatter(jnp.dot(heads_out, full_out, preferred_element_type=jnp....  34.6 us
  transfers between devices with their start and end apart: 39, of which 9 were waited for; matrix products, arithmetic and copies ran while one was open for 17% of the time, Pallas kernels for 0%

commit v1 on v0

--- a/solution.py
+++ b/solution.py
@@ -9,6 +9,12 @@
 ROPE_BASE = 10000.0
 GELU_SCALE = math.sqrt(2.0 / math.pi)
 MASKED = -1e30
+
+
+def make_the_stocks(block_here, ndim_at):
+    answer = list(block_here.shape[1:])
+    answer[ndim_at] *= block_here.shape[0]
+    return jnp.moveaxis(block_here, 0, ndim_at).reshape(answer)
 
 
 def normalize(inputs):
@@ -171,9 +177,31 @@
     gain_ffw_in = ffw_mats[3].astype(jnp.float32)
     gain_ffw_post = ffw_mats[4].astype(jnp.float32)
     mid_hat, mid_inverse = normalize(hidden)
-    ffw_rows = lax.all_gather(
-        (mid_hat * gain_ffw_in).astype(jnp.bfloat16), "tensor", axis=0, tiled=True
-    )
+
+    def check_row_in(block_in, shard_axis, pos_dim):
+        how_many = lax.axis_size(shard_axis)
+        found = tuple(((d, (d + 1) % how_many) for d in range(how_many)))
+        frames = tuple(((dev, dd) for dd, dev in found))
+        fresh, right_arr = ([], [])
+        w = 0
+        while w < how_many - 1:
+            if w % 2 == 0:
+                fresh.append(
+                    lax.ppermute(fresh[-1] if fresh else block_in, axis_name=shard_axis, perm=found)
+                )
+            else:
+                right_arr.append(
+                    lax.ppermute(
+                        right_arr[-1] if right_arr else block_in, axis_name=shard_axis, perm=frames
+                    )
+                )
+            w += 1
+        u_next = jnp.stack([*fresh[::-1], block_in, *right_arr])
+        near = lax.axis_index(shard_axis) - len(fresh)
+        u_next = u_next[(jnp.arange(how_many) - near) % how_many]
+        return make_the_stocks(u_next, pos_dim)
+
+    ffw_rows = check_row_in((mid_hat * gain_ffw_in).astype(jnp.bfloat16), "tensor", 0)
     gate = jnp.dot(ffw_rows, full_gate, preferred_element_type=jnp.float32)
     upward = jnp.dot(ffw_rows, full_up, preferred_element_type=jnp.float32)
     gelu_value, gelu_slope = gelu_parts(gate)

time: 980 us -> 976 us (level)
  waiting for transfers between devices: 258 us -> 247 us
    all_gather x1 -> x0, waiting for transfers between devices: 20.2 us -> none  [local(): lax.all_gather((mid_hat * gain_ffw_in).astype(jnp.bfloat16), 'tensor', ax...]
    ppermute x0 -> x3, waiting for transfers between devices: none -> 11.5 us  [the longest x1 7.7 us: check_row_in(): lax.ppermute(right_arr[-1] if right_arr else block_in, axis_name=shard_ax...]
  transfers between devices with their start and end apart: 39 -> 41, of which waited for: 9 -> 10; matrix products, arithmetic and copies ran while one was open for 17% -> 17% of each run, Pallas kernels for 0% -> 0%
where the time goes in v1:
time: 976 us; the launch traced here: 968 us
  blocking collectives  461 us (47%)
  waiting for transfers between devices  247 us (25%)
  starting transfers between devices  81.3 us (8%)
  matrix products  76.1 us (8%)
  local copies, waits for them, and re-layouts  48.8 us (5%)
  other arithmetic  32.7 us (3%)
  between operations  21 us (2%)
    unnamed x3, blocking collectives  351 us
    unnamed x28, starting transfers between devices  77 us
    unnamed x156, local copies, waits for them, and re-layouts  45.6 us
    all_gather x1, waiting for transfers between devices, local(): lax.all_gather(w_down, 'dp', axis=1, tiled=True)  40.7 us
    all_gather x1, waiting for transfers between devices, local(): lax.all_gather(w_up, 'dp', axis=0, tiled=True)  40.7 us
    reduce_scatter x1, waiting for transfers between devices, local(): lax.psum_scatter(contract_cols(grad_gate_in, back_gate) + contract_cols(g...  37.1 us
    reduce_scatter x1, waiting for transfers between devices, local(): lax.psum_scatter(jnp.dot(heads_out, full_out, preferred_element_type=jnp....  34.6 us
    reduce_scatter x1, waiting for transfers between devices, local(): lax.psum_scatter(jnp.dot(act, full_down, preferred_element_type=jnp.float...  33.6 us
  transfers between devices with their start and end apart: 41, of which 10 were waited for; matrix products, arithmetic and copies ran while one was open for 17% of the time, Pallas kernels for 0%

profile of v1, /device:TPU:0, one launch (start us, length us, event | category | flops | bytes accessed | tf_op | source)
XLA Modules:
  0.0 968.0 jit_solution(5206081704763167617)
XLA Ops:
  15.8 128.5 %all-reduce.27 = (bf16[1152]{0:T(1024)(128)(2,1)S(1)}, bf16[256]{0:T(256)(128)(2,1)S(1)}, bf16[256]{0:T(256)(128)(2,1)S(1)}, bf16[1152]{0:T(1024)(128)(2,1)S(1)}...) all-reduce(bf16[1152]{0:T(1024)(128)(2,1)S(1)} %dynamic-update-slic, ...), channel_id=1, replica_groups=mesh['dp'=32,'tensor'=4] {'dp'}, use_global_device_ids=true, to_apply=%add | all-reduce | flops 5120 | bytes 20480
  147.5 22.5 %all-gather.2 = bf16[32,36,256]{2,1,0:T(8,128)(2,1)S(1)} all-gather(bf16[1,36,256]{2,1,0:T(8,128)(2,1)} %bitcast.99), channel_id=1, replica_groups=mesh['dp'=32,'tensor'=4] {'dp'}, dimensions={0}, use_global_device_ids=true | all-gather | bytes 608256 | tf_op jit(solution)/shard_map/all_gather | solution.py:122
  170.2 24.3 %all-gather.1 = bf16[32,36,256]{2,1,0:T(8,128)(2,1)S(1)} all-gather(bf16[1,36,256]{2,1,0:T(8,128)(2,1)S(1)} %bitcast.100), channel_id=1, replica_groups=mesh['dp'=32,'tensor'=4] {'dp'}, dimensions={0}, use_global_device_ids=true | all-gather | bytes 608256 | tf_op jit(solution)/shard_map/all_gather | solution.py:121
  194.7 22.6 %all-gather = bf16[32,36,256]{2,1,0:T(8,128)(2,1)S(1)} all-gather(bf16[1,36,256]{2,1,0:T(8,128)(2,1)S(1)} %bitcast.101), channel_id=1, replica_groups=mesh['dp'=32,'tensor'=4] {'dp'}, dimensions={0}, use_global_device_ids=true | all-gather | bytes 608256 | tf_op jit(solution)/shard_map/all_gather | solution.py:120
  217.5 24.6 %all-gather.3 = bf16[32,36,256]{2,1,0:T(8,128)(2,1)S(1)} all-gather(bf16[1,36,256]{2,1,0:T(8,128)(2,1)S(1)} %bitcast.102), channel_id=1, replica_groups=mesh['dp'=32,'tensor'=4] {'dp'}, dimensions={0}, use_global_device_ids=true | all-gather | bytes 608256 | tf_op jit(solution)/shard_map/all_gather | solution.py:123
  254.9 34.6 %reduce-scatter.19.cloned.1.call-done = f32[160,1152]{1,0:T(8,128)} async-done(((f32[640,1152]{1,0:T(8,128)}), f32[160,1152]{1,0:T(8,128)}) %reduce-scatter.19.cloned.1.call-update) | async-done | bytes 737296 | tf_op jit(solution)/shard_map/reduce_scatter | solution.py:161
  292.6 9.0 all-gather.20.cloned.1.call-done
  301.6 7.3 reshape.221
  308.9 40.7 %all-gather.22.cloned.1.call-done = bf16[32,36,1728]{2,1,0:T(8,128)(2,1)} async-done(((bf16[1,36,1728]{2,1,0:T(8,128)(2,1)}), bf16[32,36,1728]{2,1,0:T(8,128)(2,1)}) %all-gather.22.cloned.1.call-update) | async-done | bytes 3981328 | tf_op jit(solution)/shard_map/all_gather | solution.py:171
  349.6 7.3 reshape.223
  356.8 40.7 %all-gather.24.cloned.1.call-done = bf16[32,36,1728]{2,1,0:T(8,128)(2,1)} async-done(((bf16[1,36,1728]{2,1,0:T(8,128)(2,1)}), bf16[32,36,1728]{2,1,0:T(8,128)(2,1)}) %all-gather.24.cloned.1.call-update) | async-done | bytes 3981328 | tf_op jit(solution)/shard_map/all_gather | solution.py:172
  397.5 7.3 reshape.225
  404.8 2.9 collective-permute-start.2
  408.3 7.7 collective-permute-done.2
  416.0 3.8 collective-permute-done.1
  421.2 3.2 gather_fusion
  424.4 6.5 fusion.79
  431.0 6.7 multiply_convert_fusion.1
  439.1 4.8 fusion.80
  444.2 33.6 %reduce-scatter.21.cloned.1.call-done = f32[160,1152]{1,0:T(8,128)} async-done(((f32[640,1152]{1,0:T(8,128)}), f32[160,1152]{1,0:T(8,128)}) %reduce-scatter.21.cloned.1.call-update) | async-done | bytes 737296 | tf_op jit(solution)/shard_map/reduce_scatter | solution.py:209
  481.9 25.6 %all-gather.16.cloned.1.call-done = bf16[640,1152]{1,0:T(8,128)(2,1)} async-done(((bf16[160,1152]{1,0:T(8,128)(2,1)}), bf16[640,1152]{1,0:T(8,128)(2,1)}) %all-gather.16.cloned.1.call-update) | async-done | bytes 1474576 | tf_op jit(solution)/shard_map/all_gather | solution.py:238
  507.5 10.2 %multiply_convert_fusion = (bf16[640,1728]{0,1:T(8,128)(2,1)S(1)}, bf16[640,1728]{0,1:T(8,128)(2,1)S(1)}) fusion(f32[640,1728]{0,1:T(8,128)} %copy-done.52, f32[640,1728]{0,1:T(8,128)} %get-tuple-element.90, bf16[640,1152]{1,0:T(8,128)(2,1)} %all-gather.16.cloned.1.call-done, bf16[1152,1728]{1,0:T(8,128)(2,1)} %reshape.225), kind=kOutput, calls=%fused_computation.13 | convolution fusion | flops 2573475840 | bytes 18726912 | tf_op jit(solution)/shard_map/dot_general | solution.py:70
  517.8 3.2 fusion.81
  521.5 4.9 convolution_add_fusion.2
  526.5 37.1 %reduce-scatter.23.cloned.1.call-done = f32[160,1152]{1,0:T(8,128)} async-done(((f32[640,1152]{1,0:T(8,128)}), f32[160,1152]{1,0:T(8,128)}) %reduce-scatter.23.cloned.1.call-update) | async-done | bytes 737296 | tf_op jit(solution)/shard_map/reduce_scatter | solution.py:253
  568.9 7.6 convolution_convert_fusion.2
  576.5 5.4 convolution_convert_fusion.1
  581.9 12.3 %all-gather.18.cloned.1.call-done = bf16[640,1152]{1,0:T(8,128)(2,1)} async-done(((bf16[160,1152]{1,0:T(8,128)(2,1)}), bf16[640,1152]{1,0:T(8,128)(2,1)}) %all-gather.18.cloned.1.call-update) | async-done | bytes 1474576 | tf_op jit(solution)/shard_map/all_gather | solution.py:265
  606.7 7.6 convolution_convert_fusion
  619.6 98.4 %fusion.75 = (bf16[40,256]{1,0:T(8,128)(2,1)S(1)}, bf16[40,256]{1,0:T(8,128)(2,1)S(1)}, bf16[40,256]{1,0:T(8,128)(2,1)S(1)}, bf16[40,256]{1,0:T(8,128)(2,1)S(1)}...) fusion(bf16[1152,256]{1,0:T(8,128)(2,1)S(1)} %convolution_convert_fusion.6, ...), kind=kCustom, calls=%all-reduce-scatter.7 | all-reduce-scatter fusion | flops 7946241 | bytes 14800384
  720.7 5.6 collective-permute-start.26
  728.5 5.3 collective-permute-start.10
  733.8 3.0 collective-permute-start.14
  736.9 5.2 collective-permute-start.18
  745.5 5.1 collective-permute-start.9
  750.7 4.0 collective-permute-start.8
  756.2 3.3 collective-permute-start.13
  759.5 3.7 collective-permute-start.12
  763.2 2.5 collective-permute-start.17
  765.8 3.7 collective-permute-start.16
  774.8 2.5 collective-permute-start.11
  779.3 2.5 collective-permute-start.20
  790.4 2.5 collective-permute-start.23
  794.4 2.9 collective-permute-start.28
  802.8 2.5 concatenate.23
  805.8 3.2 concatenate.24
  812.7 123.9 %all-reduce.26 = (bf16[1152]{0:T(1024)(128)(2,1)S(1)}, bf16[1152]{0:T(1024)(128)(2,1)S(1)}, bf16[1152]{0:T(1024)(128)(2,1)S(1)}, bf16[1152]{0:T(1024)(128)(2,1)S...) all-reduce(bf16[1152]{0:T(1024)(128)(2,1)S(1)} %get-tuple-element.2, ...), channel_id=13, replica_groups=mesh['dp'=32,'tensor'=4] {'dp'}, use_global_device_ids=true, to_apply=%region_29.30.clone | all-reduce | flops 5120 | bytes 20480
  937.0 16.3 %all-reduce.28 = (bf16[36,256]{1,0:T(8,128)(2,1)S(1)}, bf16[36,256]{1,0:T(8,128)(2,1)S(1)}, bf16[36]{0:T(256)(128)(2,1)S(1)}, bf16[36]{0:T(256)(128)(2,1)S(1)}, ...) all-reduce(bf16[36,256]{1,0:T(8,128)(2,1)S(1)} %constant_dynamic-sl, ...), channel_id=1, replica_groups=mesh['dp'=32,'tensor'=4] {'tensor'}, use_global_device_ids=true, to_apply=%region_21.22 | all-reduce | flops 18592 | bytes 74368 | tf_op jit(solution)/shard_map/psum | solution.py:334
  (297 shorter events, 98.1 us)
Async XLA Ops:
  8.0 162.2 %copy-start.40 = (bf16[36,256]{1,0:T(8,128)(2,1)S(1)}, bf16[36,256]{1,0:T(8,128)(2,1)}, u32[]{:S(2)}) copy-start(bf16[36,256]{1,0:T(8,128)(2,1)} %param.22) | copy-start | bytes 55300
  8.0 234.3 %all-gather.14.cloned.1.call-start = ((), (), s32[]{:S(2)}) async-start(), calls=%async_computation.4 | async-start | bytes 1843200 | tf_op jit(solution)/shard_map/all_gather | solution.py:140
  147.5 142.0 %reduce-scatter.19.cloned.1.call-start = ((), (), s32[]{:S(2)}) async-start(), calls=%async_computation.5 | async-start | bytes 3686400 | tf_op jit(solution)/shard_map/reduce_scatter | solution.py:161
  170.2 78.1 %copy-start.20 = (bf16[1152,256]{1,0:T(8,128)(2,1)}, bf16[1152,256]{1,0:T(8,128)(2,1)S(1)}, u32[]{:S(2)}) copy-start(bf16[1152,256]{1,0:T(8,128)(2,1)S(1)} %reshape.217) | copy-start | bytes 1769476
  194.6 49.9 %copy-start.11 = (bf16[1152,256]{1,0:T(8,128)(2,1)}, bf16[1152,256]{1,0:T(8,128)(2,1)S(1)}, u32[]{:S(2)}) copy-start(bf16[1152,256]{1,0:T(8,128)(2,1)S(1)} %reshape.215) | copy-start | bytes 1769476
  194.7 47.5 %copy-start.46 = (s32[1,640]{1,0:T(1,128)S(1)}, s32[1,640]{1,0:T(1,128)}, u32[]{:S(2)}) copy-start(s32[1,640]{1,0:T(1,128)} %param.19) | copy-start | bytes 7684
  194.7 47.6 %copy-start.47 = (s32[1,640]{1,0:T(1,128)S(1)}, s32[1,640]{1,0:T(1,128)}, u32[]{:S(2)}) copy-start(s32[1,640]{1,0:T(1,128)} %param.20) | copy-start | bytes 7684
  194.7 50.7 %copy-start.44 = (f32[256]{0:T(256)}, f32[256]{0:T(256)S(1)}, u32[]{:S(2)}) copy-start(f32[256]{0:T(256)S(1)} %convert_element_type.184) | copy-start | bytes 3076
  253.1 48.5 %all-gather.20.cloned.1.call-start = ((), (), s32[]{:S(2)}) async-start(), calls=%async_computation.11 | async-start | bytes 4730880 | tf_op jit(solution)/shard_map/all_gather | solution.py:170
  253.6 95.9 %all-gather.22.cloned.1.call-start = ((), (), s32[]{:S(2)}) async-start(), calls=%async_computation.12 | async-start | bytes 4730880 | tf_op jit(solution)/shard_map/all_gather | solution.py:171
  254.2 143.3 %all-gather.24.cloned.1.call-start = ((), (), s32[]{:S(2)}) async-start(), calls=%async_computation.13 | async-start | bytes 4730880 | tf_op jit(solution)/shard_map/all_gather | solution.py:172
  254.8 223.1 %reduce-scatter.21.cloned.1.call-start = ((), (), s32[]{:S(2)}) async-start(), calls=%async_computation.6 | async-start | bytes 3686400 | tf_op jit(solution)/shard_map/reduce_scatter | solution.py:209
  292.4 115.4 %collective-permute-start = (bf16[160,1152]{1,0:T(8,128)(2,1)S(1)}, bf16[160,1152]{1,0:T(8,128)(2,1)S(1)}, u32[]{:S(2)}, u32[]{:S(2)}) collective-permute-start(bf16[160,1152]{1,0:T(8,128)(2,1)S(1)} %multiply_convert_fusion.4), channel_id=1, source_target_pairs={{0,1},{1,2},{2,3},{3,0},{4,5},{5,6},{6,7},{7,4},{8,9},{9,10},{10,1... | collective-permute-start | bytes 1105928 | tf_op jit(solution)/shard_map/ppermute | solution.py:190
  404.8 11.2 %collective-permute-start.2 = (bf16[160,1152]{1,0:T(8,128)(2,1)S(1)}, bf16[160,1152]{1,0:T(8,128)(2,1)S(1)}, u32[]{:S(2)}, u32[]{:S(2)}) collective-permute-start(bf16[160,1152]{1,0:T(8,128)(2,1)S(1)} %multiply_convert_fusion.4), channel_id=1, source_target_pairs={{1,0},{2,1},{3,2},{0,3},{5,4},{6,5},{7,6},{4,7},{9,8},{10,9},{11,1... | collective-permute-start | bytes 1105928 | tf_op jit(solution)/shard_map/ppermute | solution.py:194
  407.8 12.0 %collective-permute-start.1 = (bf16[160,1152]{1,0:T(8,128)(2,1)S(1)}, bf16[160,1152]{1,0:T(8,128)(2,1)S(1)}, u32[]{:S(2)}, u32[]{:S(2)}) collective-permute-start(bf16[160,1152]{1,0:T(8,128)(2,1)S(1)} %collective-permute-done), channel_id=1, source_target_pairs={{0,1},{1,2},{2,3},{3,0},{4,5},{5,6},{6,7},{7,4},{8,9},{9,10},{10,1... | collective-permute-start | bytes 1105928 | tf_op jit(solution)/shard_map/ppermute | solution.py:190
  444.0 63.5 %all-gather.16.cloned.1.call-start = ((), (), s32[]{:S(2)}) async-start(), calls=%async_computation.7 | async-start | bytes 1843200 | tf_op jit(solution)/shard_map/all_gather | solution.py:238
  481.9 81.7 %reduce-scatter.23.cloned.1.call-start = ((), (), s32[]{:S(2)}) async-start(), calls=%async_computation.8 | async-start | bytes 3686400 | tf_op jit(solution)/shard_map/reduce_scatter | solution.py:253
  526.4 67.8 %all-gather.18.cloned.1.call-start = ((), (), s32[]{:S(2)}) async-start(), calls=%async_computation.9 | async-start | bytes 1843200 | tf_op jit(solution)/shard_map/all_gather | solution.py:265
  568.6 242.7 %reduce-scatter.25.cloned.1.call-start = ((), (), s32[]{:S(2)}) async-start(), calls=%async_computation.10 | async-start | bytes 1843200 | tf_op jit(solution)/shard_map/reduce_scatter | solution.py:293
  718.1 36.6 %collective-permute-start.5 = (bf16[40,256]{1,0:T(8,128)(2,1)S(1)}, bf16[40,256]{1,0:T(8,128)(2,1)S(1)}, u32[]{:S(2)}, u32[]{:S(2)}) collective-permute-start(bf16[40,256]{1,0:T(8,128)(2,1)S(1)} %get-tuple-element.54), channel_id=1, source_target_pairs={{0,12},{4,16},{8,20},{12,24},{16,28},{20,32},{24,36},{28,40},{32,4... | collective-permute-start | bytes 61448
  719.4 26.1 %collective-permute-start.22 = (bf16[4,1728]{1,0:T(4,128)(2,1)S(1)}, bf16[4,1728]{1,0:T(4,128)(2,1)S(1)}, u32[]{:S(2)}, u32[]{:S(2)}) collective-permute-start(bf16[4,1728]{1,0:T(4,128)(2,1)S(1)} %slice.46), channel_id=1, source_target_pairs={{0,16},{4,20},{8,24},{12,28},{16,32},{20,36},{24,40},{28,44},{32,4... | collective-permute-start | bytes 41480
  720.7 30.0 %collective-permute-start.26 = (bf16[4,1728]{1,0:T(4,128)(2,1)S(1)}, bf16[4,1728]{1,0:T(4,128)(2,1)}, u32[]{:S(2)}, u32[]{:S(2)}) collective-permute-start(bf16[4,1728]{1,0:T(4,128)(2,1)S(1)} %slice.47), channel_id=1, source_target_pairs={{0,16},{4,20},{8,24},{12,28},{16,32},{20,36},{24,40},{28,44},{32,4... | collective-permute-start | bytes 41480
  726.3 7.5 collective-permute-start.6
  728.5 8.3 collective-permute-start.10
  733.8 8.2 collective-permute-start.14
  736.9 6.5 collective-permute-start.18
  742.1 14.1 %collective-permute-start.4 = (bf16[40,256]{1,0:T(8,128)(2,1)S(1)}, bf16[40,256]{1,0:T(8,128)(2,1)S(1)}, u32[]{:S(2)}, u32[]{:S(2)}) collective-permute-start(bf16[40,256]{1,0:T(8,128)(2,1)S(1)} %get-tuple-element.54), channel_id=1, source_target_pairs={{0,8},{4,12},{8,16},{12,20},{16,24},{20,28},{24,32},{28,36},{32,40... | collective-permute-start | bytes 61448
  743.4 16.1 %collective-permute-start.3 = (bf16[40,256]{1,0:T(8,128)(2,1)S(1)}, bf16[40,256]{1,0:T(8,128)(2,1)S(1)}, u32[]{:S(2)}, u32[]{:S(2)}) collective-permute-start(bf16[40,256]{1,0:T(8,128)(2,1)S(1)} %get-tuple-element.54), channel_id=1, source_target_pairs={{0,4},{4,8},{8,12},{12,16},{16,20},{20,24},{24,28},{28,32},{32,36}... | collective-permute-start | bytes 61448
  745.5 17.7 %collective-permute-start.9 = (bf16[40,256]{1,0:T(8,128)(2,1)S(1)}, bf16[40,256]{1,0:T(8,128)(2,1)S(1)}, u32[]{:S(2)}, u32[]{:S(2)}) collective-permute-start(bf16[40,256]{1,0:T(8,128)(2,1)S(1)} %get-tuple-element.55), channel_id=1, source_target_pairs={{0,12},{4,16},{8,20},{12,24},{16,28},{20,32},{24,36},{28,40},{32,4... | collective-permute-start | bytes 61448
  750.7 15.1 %collective-permute-start.8 = (bf16[40,256]{1,0:T(8,128)(2,1)S(1)}, bf16[40,256]{1,0:T(8,128)(2,1)S(1)}, u32[]{:S(2)}, u32[]{:S(2)}) collective-permute-start(bf16[40,256]{1,0:T(8,128)(2,1)S(1)} %get-tuple-element.55), channel_id=1, source_target_pairs={{0,8},{4,12},{8,16},{12,20},{16,24},{20,28},{24,32},{28,36},{32,40... | collective-permute-start | bytes 61448
  754.7 14.8 %collective-permute-start.7 = (bf16[40,256]{1,0:T(8,128)(2,1)S(1)}, bf16[40,256]{1,0:T(8,128)(2,1)S(1)}, u32[]{:S(2)}, u32[]{:S(2)}) collective-permute-start(bf16[40,256]{1,0:T(8,128)(2,1)S(1)} %get-tuple-element.55), channel_id=1, source_target_pairs={{0,4},{4,8},{8,12},{12,16},{16,20},{20,24},{24,28},{28,32},{32,36}... | collective-permute-start | bytes 61448
  756.2 18.7 %collective-permute-start.13 = (bf16[40,256]{1,0:T(8,128)(2,1)S(1)}, bf16[40,256]{1,0:T(8,128)(2,1)S(1)}, u32[]{:S(2)}, u32[]{:S(2)}) collective-permute-start(bf16[40,256]{1,0:T(8,128)(2,1)S(1)} %get-tuple-element.56), channel_id=1, source_target_pairs={{0,12},{4,16},{8,20},{12,24},{16,28},{20,32},{24,36},{28,40},{32,4... | collective-permute-start | bytes 61448
  759.5 17.9 %collective-permute-start.12 = (bf16[40,256]{1,0:T(8,128)(2,1)S(1)}, bf16[40,256]{1,0:T(8,128)(2,1)S(1)}, u32[]{:S(2)}, u32[]{:S(2)}) collective-permute-start(bf16[40,256]{1,0:T(8,128)(2,1)S(1)} %get-tuple-element.56), channel_id=1, source_target_pairs={{0,8},{4,12},{8,16},{12,20},{16,24},{20,28},{24,32},{28,36},{32,40... | collective-permute-start | bytes 61448
  763.2 16.1 %collective-permute-start.17 = (bf16[40,256]{1,0:T(8,128)(2,1)S(1)}, bf16[40,256]{1,0:T(8,128)(2,1)S(1)}, u32[]{:S(2)}, u32[]{:S(2)}) collective-permute-start(bf16[40,256]{1,0:T(8,128)(2,1)S(1)} %get-tuple-element.57), channel_id=1, source_target_pairs={{0,12},{4,16},{8,20},{12,24},{16,28},{20,32},{24,36},{28,40},{32,4... | collective-permute-start | bytes 61448
  765.8 16.0 %collective-permute-start.16 = (bf16[40,256]{1,0:T(8,128)(2,1)S(1)}, bf16[40,256]{1,0:T(8,128)(2,1)S(1)}, u32[]{:S(2)}, u32[]{:S(2)}) collective-permute-start(bf16[40,256]{1,0:T(8,128)(2,1)S(1)} %get-tuple-element.57), channel_id=1, source_target_pairs={{0,8},{4,12},{8,16},{12,20},{16,24},{20,28},{24,32},{28,36},{32,40... | collective-permute-start | bytes 61448
  769.5 14.1 %collective-permute-start.15 = (bf16[40,256]{1,0:T(8,128)(2,1)S(1)}, bf16[40,256]{1,0:T(8,128)(2,1)S(1)}, u32[]{:S(2)}, u32[]{:S(2)}) collective-permute-start(bf16[40,256]{1,0:T(8,128)(2,1)S(1)} %get-tuple-element.57), channel_id=1, source_target_pairs={{0,4},{4,8},{8,12},{12,16},{16,20},{20,24},{24,28},{28,32},{32,36}... | collective-permute-start | bytes 61448
  774.8 12.2 %collective-permute-start.11 = (bf16[40,256]{1,0:T(8,128)(2,1)S(1)}, bf16[40,256]{1,0:T(8,128)(2,1)S(1)}, u32[]{:S(2)}, u32[]{:S(2)}) collective-permute-start(bf16[40,256]{1,0:T(8,128)(2,1)S(1)} %get-tuple-element.56), channel_id=1, source_target_pairs={{0,4},{4,8},{8,12},{12,16},{16,20},{20,24},{24,28},{28,32},{32,36}... | collective-permute-start | bytes 61448
  777.4 13.0 %collective-permute-start.21 = (bf16[40,1728]{1,0:T(8,128)(2,1)S(1)}, bf16[40,1728]{1,0:T(8,128)(2,1)S(1)}, u32[]{:S(2)}, u32[]{:S(2)}) collective-permute-start(bf16[40,1728]{1,0:T(8,128)(2,1)S(1)} %get-tuple-element.58), channel_id=1, source_target_pairs={{0,12},{4,16},{8,20},{12,24},{16,28},{20,32},{24,36},{28,40},{32,4... | collective-permute-start | bytes 414728
  779.3 13.6 %collective-permute-start.20 = (bf16[40,1728]{1,0:T(8,128)(2,1)S(1)}, bf16[40,1728]{1,0:T(8,128)(2,1)S(1)}, u32[]{:S(2)}, u32[]{:S(2)}) collective-permute-start(bf16[40,1728]{1,0:T(8,128)(2,1)S(1)} %get-tuple-element.58), channel_id=1, source_target_pairs={{0,8},{4,12},{8,16},{12,20},{16,24},{20,28},{24,32},{28,36},{32,40... | collective-permute-start | bytes 414728
  781.8 12.6 %collective-permute-start.19 = (bf16[40,1728]{1,0:T(8,128)(2,1)S(1)}, bf16[40,1728]{1,0:T(8,128)(2,1)S(1)}, u32[]{:S(2)}, u32[]{:S(2)}) collective-permute-start(bf16[40,1728]{1,0:T(8,128)(2,1)S(1)} %get-tuple-element.58), channel_id=1, source_target_pairs={{0,4},{4,8},{8,12},{12,16},{16,20},{20,24},{24,28},{28,32},{32,36}... | collective-permute-start | bytes 414728
  783.5 13.7 %collective-permute-start.25 = (bf16[40,1728]{1,0:T(8,128)(2,1)S(1)}, bf16[40,1728]{1,0:T(8,128)(2,1)S(1)}, u32[]{:S(2)}, u32[]{:S(2)}) collective-permute-start(bf16[40,1728]{1,0:T(8,128)(2,1)S(1)} %get-tuple-element.59), channel_id=1, source_target_pairs={{0,12},{4,16},{8,20},{12,24},{16,28},{20,32},{24,36},{28,40},{32,4... | collective-permute-start | bytes 414728
  787.1 13.4 %collective-permute-start.24 = (bf16[40,1728]{1,0:T(8,128)(2,1)S(1)}, bf16[40,1728]{1,0:T(8,128)(2,1)S(1)}, u32[]{:S(2)}, u32[]{:S(2)}) collective-permute-start(bf16[40,1728]{1,0:T(8,128)(2,1)S(1)} %get-tuple-element.59), channel_id=1, source_target_pairs={{0,8},{4,12},{8,16},{12,20},{16,24},{20,28},{24,32},{28,36},{32,40... | collective-permute-start | bytes 414728
  790.4 12.4 %collective-permute-start.23 = (bf16[40,1728]{1,0:T(8,128)(2,1)S(1)}, bf16[40,1728]{1,0:T(8,128)(2,1)}, u32[]{:S(2)}, u32[]{:S(2)}) collective-permute-start(bf16[40,1728]{1,0:T(8,128)(2,1)S(1)} %get-tuple-element.59), channel_id=1, source_target_pairs={{0,4},{4,8},{8,12},{12,16},{16,20},{20,24},{24,28},{28,32},{32,36}... | collective-permute-start | bytes 414728
  792.9 12.4 %collective-permute-start.29 = (bf16[40,1728]{1,0:T(8,128)(2,1)S(1)}, bf16[40,1728]{1,0:T(8,128)(2,1)S(1)}, u32[]{:S(2)}, u32[]{:S(2)}) collective-permute-start(bf16[40,1728]{1,0:T(8,128)(2,1)S(1)} %get-tuple-element.60), channel_id=1, source_target_pairs={{0,12},{4,16},{8,20},{12,24},{16,28},{20,32},{24,36},{28,40},{32,4... | collective-permute-start | bytes 414728
  794.4 10.9 %collective-permute-start.28 = (bf16[40,1728]{1,0:T(8,128)(2,1)S(1)}, bf16[40,1728]{1,0:T(8,128)(2,1)}, u32[]{:S(2)}, u32[]{:S(2)}) collective-permute-start(bf16[40,1728]{1,0:T(8,128)(2,1)S(1)} %get-tuple-element.60), channel_id=1, source_target_pairs={{0,8},{4,12},{8,16},{12,20},{16,24},{20,28},{24,32},{28,36},{32,40... | collective-permute-start | bytes 414728
  797.3 8.6 collective-permute-start.27
  800.5 4.7 collective-permute-start.30
  802.7 155.0 %copy-start.7 = (f32[160,1152]{1,0:T(8,128)S(1)}, f32[160,1152]{1,0:T(8,128)}, u32[]{:S(2)}) copy-start(f32[160,1152]{1,0:T(8,128)} %copy-done.6) | copy-start | bytes 2211844
  (50 other events, 398.6 us)
Sparse Core Ops, SparseCore 0:
  147.6 23.1 all-gather.13
  253.2 36.2 reduce-scatter.18
  444.1 33.6 reduce-scatter.20
  482.0 25.4 all-gather.15
  526.6 36.9 reduce-scatter.22
  568.8 25.4 all-gather.17
  606.8 25.5 reduce-scatter.24
Sparse Core Ops, SparseCore 1:
  255.9 45.7 all-gather.19
  303.8 45.7 all-gather.21
  351.8 45.7 all-gather.23
